TPU v7x, 128 devices: a whole 4x4x4 slice. The times are simulated.
128 devices in a mesh: dp: 8 (over z, core), tensor: 16 (over x, y).
Axes of the slice: x: 4, y: 4, z: 4, core: 2. Of those that a mesh axis runs over, the one named last changes fastest.
Arguments:
- queries: bfloat16 [4096, 36864], P('dp', 'tensor'), may hold values from -6.8560344 to 6.8560344
- cache: bfloat16 [8, 3072, 576], P('dp', 'tensor'), may hold values from -4 to 4
- offsets: int32 [8], P('dp'), may hold values from 0 to 2560, as said below
- value_up: bfloat16 [64, 512, 128], P('tensor'), may hold values from -0.25 to 0.25
- out_proj: bfloat16 [8192, 3584], P('tensor', 'dp'), may hold values from -0.0625 to 0.0625
- resid: bfloat16 [4096, 3584], P(('dp', 'tensor')), may hold values from -3 to 3
- norm_gain: float32 [3584], replicated, may hold values from 0.25 to 1.75
- routes: int32 [4096, 8], P(('dp', 'tensor')), may hold values from 0 to 127, as said below
- route_weights: float32 [4096, 8], P(('dp', 'tensor')), may hold values from 0.1 to 0.6
- expert_in: bfloat16 [128, 3584, 2048], P(('dp', 'tensor')), may hold values from -0.09375 to 0.09375
- expert_down: bfloat16 [128, 1024, 3584], P(('dp', 'tensor')), may hold values from -0.1875 to 0.1875
Outputs:
- mixed: bfloat16 [4096, 3584], P(('dp', 'tensor'))
Inputs may be any that keep to these rules, and one draw needn't show every extreme that they name: `routes`: each row names 8 different experts. Among the 32 rows of one device (aligned blocks of rows) a quarter of the experts is named 4 times, a quarter 3 times, a quarter once and a quarter never; in every draw one expert is named 4 times in every block. `offsets`: some sequence's offset is 2560; the new tokens' own latents are in the cache at their positions.
All inputs are finite; a program needn't handle non-finite values.
Results may differ from a plain program's by a relative error of at most 0.024.
Values may be sent and summed in bfloat16 or wider, within the bound.
A program may use at most 192 MiB of HBM per device.

v0:
```python
import jax
import jax.numpy as jnp
from jax import lax
from jax.sharding import PartitionSpec as P


def shards(
    queries,
    cache,
    offsets,
    value_up,
    out_proj,
    resid,
    norm_gain,
    routes,
    route_weights,
    expert_in,
    expert_down,
):
    heads_dev = value_up.shape[0]
    latent_width = value_up.shape[1]
    key_width = cache.shape[2]
    tok_grp = queries.shape[0]
    score_scale = (value_up.shape[2] + key_width - latent_width) ** (-0.5)
    query_heads = queries.reshape(tok_grp, heads_dev, key_width)
    start_pos = offsets[0]
    query_pos = start_pos + jnp.arange(tok_grp, dtype=jnp.int32)
    running = jnp.full((heads_dev, tok_grp), -1e30, jnp.float32)
    key_rows = lax.all_gather(cache, "tensor", axis=1, tiled=True)[0]
    key_count = key_rows.shape[0]
    scores = (
        jnp.einsum("thc,kc->htk", query_heads, key_rows, preferred_element_type=jnp.float32)
        * score_scale
    )
    key_pos = jnp.arange(key_count, dtype=jnp.int32)
    visible = key_pos[None, :] <= query_pos[:, None]
    scores = jnp.where(visible[None], scores, jnp.float32(-1e30))
    highest = jnp.maximum(running, jnp.max(scores, axis=2))
    weights = jnp.where(visible[None], jnp.exp(scores - highest[..., None]), jnp.float32(0.0))
    totals = jnp.sum(weights, axis=2)
    weighted = jnp.einsum(
        "htk,kc->htc",
        weights.astype(jnp.bfloat16),
        key_rows[:, :latent_width],
        preferred_element_type=jnp.float32,
    )
    running, totals, weighted = (highest, totals, weighted)
    context = (weighted / totals[..., None]).astype(jnp.bfloat16)
    head_out = jnp.einsum("htc,hcv->thv", context, value_up, preferred_element_type=jnp.float32)
    head_out = head_out.astype(jnp.bfloat16).reshape(tok_grp, -1)
    partial_value = jnp.dot(
        head_out,
        lax.all_gather(out_proj, "dp", axis=1, tiled=True),
        preferred_element_type=jnp.float32,
    )
    tok_dev = resid.shape[0]
    summed_all = lax.psum(partial_value.astype(jnp.bfloat16), "tensor").astype(jnp.float32)
    attn_rows = lax.dynamic_slice_in_dim(summed_all, lax.axis_index("tensor") * tok_dev, tok_dev, 0)
    stream = resid.astype(jnp.float32) + attn_rows
    mean_square = jnp.mean(stream * stream, axis=1, keepdims=True)
    normed = (stream * lax.rsqrt(mean_square + 1e-06) * norm_gain).astype(jnp.bfloat16)
    experts = lax.axis_size("dp") * lax.axis_size("tensor")
    top_count = routes.shape[1]
    capacity = 2 * tok_dev * top_count // experts
    d_model = normed.shape[1]
    hidden_units = expert_down.shape[1]
    flat_ids = routes.reshape(-1)
    onehot = (flat_ids[:, None] == jnp.arange(experts, dtype=jnp.int32)[None, :]).astype(jnp.int32)
    slot_rank = jnp.sum(onehot * (jnp.cumsum(onehot, axis=0) - 1), axis=1)
    slot_index = flat_ids * capacity + slot_rank
    slot_ids = jnp.arange(experts * capacity, dtype=jnp.int32)
    placing = jnp.any(
        slot_ids[:, None, None] == slot_index.reshape(tok_dev, top_count)[None], axis=2
    )
    outgoing = jnp.dot(placing.astype(jnp.bfloat16), normed, preferred_element_type=jnp.float32)
    outgoing = outgoing.astype(jnp.bfloat16).reshape(experts, capacity, d_model)
    row_block = lax.all_to_all(outgoing, ("dp", "tensor"), split_axis=0, concat_axis=0, tiled=True)
    row_shape = row_block.shape
    flat_rows = row_block.reshape(-1, row_shape[-1])
    joint_proj = jnp.dot(flat_rows, expert_in[0], preferred_element_type=jnp.float32)
    hidden = (jax.nn.silu(joint_proj[:, :hidden_units]) * joint_proj[:, hidden_units:]).astype(
        jnp.bfloat16
    )
    expert_out = jnp.dot(hidden, expert_down[0], preferred_element_type=jnp.float32).astype(
        jnp.bfloat16
    )
    returned = lax.all_to_all(
        expert_out.reshape(row_shape), ("dp", "tensor"), split_axis=0, concat_axis=0, tiled=True
    )
    results = returned.reshape(experts * capacity, d_model)
    picked = results[slot_index].reshape(tok_dev, top_count, d_model)
    routed_sum = jnp.einsum("tk,tkd->td", route_weights, picked.astype(jnp.float32))
    return (stream + routed_sum).astype(jnp.bfloat16)


def solution(mesh):
    return jax.shard_map(
        shards,
        mesh=mesh,
        in_specs=(
            P("dp", "tensor"),
            P("dp", "tensor", None),
            P("dp"),
            P("tensor", None, None),
            P("tensor", "dp"),
            P(("dp", "tensor"), None),
            P(),
            P(("dp", "tensor"), None),
            P(("dp", "tensor"), None),
            P(("dp", "tensor"), None, None),
            P(("dp", "tensor"), None, None),
        ),
        out_specs=P(("dp", "tensor"), None),
        check_vma=False,
    )
```

profile of v0, /device:TPU:1, one launch (start us, length us, event | category | flops | bytes accessed | tf_op | source)
XLA Modules:
  0.0 396.2 jit_solution(15991651440541174260)
XLA Ops:
  6.5 0.0 copy-start
  6.5 0.0 all-gather.3.cloned.1.call-start
  6.5 0.7 all-gather.3.cloned.1.call-update
  7.3 0.0 all-gather.5.cloned.1.call-start
  7.3 0.7 all-gather.5.cloned.1.call-update
  8.0 0.0 all-reduce.2.cloned.1.call-start
  8.7 1.3 iota_compare_fusion
  10.0 4.3 %copy.35 = bf16[512,2304]{0,1:T(8,128)(2,1)} copy(bf16[512,2304]{1,0:T(8,128)(2,1)} %param.11) | data formatting | bytes 4718592 | tf_op args[0]
  14.3 48.7 %all-gather.3.cloned.1.call-done = bf16[1,3072,576]{2,1,0:T(8,128)(2,1)} async-done(((bf16[1,192,576]{2,1,0:T(8,128)(2,1)}), bf16[1,3072,576]{2,1,0:T(8,128)(2,1)}) %all-gather.3.cloned.1.call-update) | async-done | bytes 3538960 | tf_op jit(solution)/shard_map/all_gather | solution.py:29
  63.0 18.4 %fusion = (f32[4,512]{1,0:T(4,128)S(1)}, f32[3072,512,4]{1,0,2:T(8,128)}) fusion(pred[512,3072]{0,1:T(8,128)(4,1)S(1)} %iota_compare_fusion, bf16[512,4,576]{0,2,1:T(8,128)(2,1)} %bitcast.61, bf16[1,3072,576]{2,1,0:T(8,128)(2,1)} %all-gather.3.cloned.1.call-done), kind=kOutput, calls=%fused_computation.3 | convolution fusion | flops 7266629632 | bytes 32645120 | tf_op jit(solution)/shard_map/thc,kc->htk/dot_general | solution.py:32
  81.4 6.1 %copy.34 = bf16[1,3072,576]{1,2,0:T(8,128)(2,1)} copy(bf16[1,3072,576]{2,1,0:T(8,128)(2,1)} %all-gather.3.cloned.1.call-done) | data formatting | bytes 7077888 | tf_op jit(solution)/shard_map/all_gather | solution.py:29
  87.5 11.7 %fusion.1 = f32[4,512]{1,0:T(4,128)S(1)} fusion(f32[3072,512,4]{1,0,2:T(8,128)} %get-tuple-element.8, f32[4,512]{1,0:T(4,128)S(1)} %broadcast_maximum_fusion, pred[512,3072]{0,1:T(8,128)(4,1)S(1)} %iota_compare_fusion), kind=kLoop, calls=%fused_computation.4 | loop fusion | flops 31455232 | bytes 26755072 | tf_op jit(solution)/shard_map/reduce_sum | solution.py:40
  99.2 14.4 %fusion.5 = f32[4,512,512]{2,1,0:T(8,128)} fusion(f32[3072,512,4]{1,0,2:T(8,128)} %get-tuple-element.8, f32[4,512]{1,0:T(4,128)S(1)} %broadcast_maximum_fusion, pred[512,3072]{0,1:T(8,128)(4,1)S(1)} %iota_compare_fusion, bf16[3072,576]{0,1:T(8,128)(2,1)} %bitcast.60), kind=kOutput, calls=%fused_computation.8 | convolution fusion | flops 6473908224 | bytes 34086912 | tf_op jit(solution)/shard_map/htk,kc->htc/dot_general | solution.py:41
  113.7 0.0 copy-done
  113.7 3.1 fusion.19
  116.8 0.0 all-gather.5.cloned.1.call-done
  116.8 0.0 copy-start.4
  116.8 6.0 %convolution_convert_fusion.1 = bf16[512,3584]{1,0:T(8,128)(2,1)} fusion(bf16[512,512]{0,1:T(8,128)(2,1)S(1)} %bitcast.65, bf16[512,3584]{0,1:T(8,128)(2,1)} %all-gather.5.cloned.1.call-done), kind=kOutput, calls=%fused_computation.15 | convolution fusion | flops 1880883200 | bytes 7864320 | tf_op jit(solution)/shard_map/dot_general | solution.py:51
  122.8 0.0 all-reduce.2.cloned.1.call-update
  122.8 0.0 copy-done.4
  122.9 0.1 copy.39
  122.9 0.1 eq.43
  123.0 0.1 eq.39
  123.1 0.1 copy.42
  123.2 0.2 fusion.27
  123.5 0.1 add_add_fusion
  123.6 0.2 fusion.28
  123.8 0.1 reduce_sum.33
  123.9 0.2 fusion.22
  124.1 97.0 %all-reduce.2.cloned.1.call-done = bf16[512,3584]{1,0:T(8,128)(2,1)} async-done(((bf16[512,3584]{1,0:T(8,128)(2,1)}), bf16[512,3584]{1,0:T(8,128)(2,1)}) %all-reduce.2.cloned.1.call-update) | async-done | bytes 3670032 | tf_op jit(solution)/shard_map/psum | solution.py:57
  221.1 0.0 copy-done.2
  221.1 1.1 multiply_reduce_fusion
  222.3 4.0 %convolution_convert_fusion = bf16[512,3584]{1,0:T(8,128)(2,1)} fusion(pred[512,32]{0,1:T(8,128)(4,1)S(1)} %fusion.22, bf16[32,3584]{1,0:T(8,128)(2,1)S(1)} %copy-done.2, f32[3584]{0:T(1024)S(1)} %copy-done.3, f32[32]{0:T(128)S(1)} %add_rsqrt_fusion, bf16[512,3584]{1,0:T(8,128)(2,1)} %all-reduce.2.cloned.1.call-done, s32[]{:T(128)S(6)} %select_n.22), kind=kOutput, calls=%fused_computation.14 | convolution fusion | flops 119963648 | bytes 4159620 | tf_op jit(solution)/shard_map/dot_general | solution.py:75
  226.3 7.0 %reshape.114 = bf16[128,4,3584]{2,1,0:T(4,128)(2,1)} reshape(bf16[512,3584]{1,0:T(8,128)(2,1)} %convolution_convert_fusion) | data formatting | bytes 7340032 | tf_op jit(solution)/shard_map/reshape | solution.py:76
  233.3 55.2 %all_to_all.10 = bf16[128,4,3584]{2,1,0:T(4,128)(2,1)} all-to-all(bf16[128,4,3584]{2,1,0:T(4,128)(2,1)} %reshape.114), channel_id=1, replica_groups=mesh['dp'=8,'tensor'=16] {'dp','tensor'}, dimensions={0} | all-to-all | bytes 7340032 | tf_op jit(solution)/shard_map/all_to_all | solution.py:77
  288.5 6.7 %reshape.115 = bf16[512,3584]{1,0:T(8,128)(2,1)} reshape(bf16[128,4,3584]{2,1,0:T(4,128)(2,1)} %all_to_all.10) | data formatting | bytes 7340032 | tf_op jit(solution)/shard_map/reshape | solution.py:79
  295.3 12.1 %fusion.3 = f32[512,2048]{1,0:T(8,128)S(1)} fusion(bf16[512,3584]{1,0:T(8,128)(2,1)} %reshape.115, bf16[1,3584,2048]{2,1,0:T(8,128)(2,1)} %param.20), kind=kOutput, calls=%fused_computation.6 | convolution fusion | flops 7516192768 | bytes 22544384 | tf_op jit(solution)/shard_map/dot_general | solution.py:80
  307.3 8.7 %fusion.10 = bf16[512,3584]{1,0:T(8,128)(2,1)} fusion(bf16[1,1024,3584]{2,1,0:T(8,128)(2,1)} %param.21, f32[512,2048]{1,0:T(8,128)S(1)} %fusion.3), kind=kOutput, calls=%fused_computation.13 | convolution fusion | flops 3763077120 | bytes 15204352 | tf_op jit(solution)/shard_map/dot_general | solution.py:84
  316.0 7.0 %reshape.116 = bf16[128,4,3584]{2,1,0:T(4,128)(2,1)} reshape(bf16[512,3584]{1,0:T(8,128)(2,1)} %fusion.10) | data formatting | bytes 7340032 | tf_op jit(solution)/shard_map/reshape | solution.py:88
  323.0 5.0 %all-to-all-start.1 = ((bf16[128,4,3584]{2,1,0:T(4,128)(2,1)}), bf16[128,4,3584]{2,1,0:T(4,128)(2,1)}, u32[]{:S(2)}, u32[]{:S(2)}) async-start(bf16[128,4,3584]{2,1,0:T(4,128)(2,1)} %reshape.116), calls=%async_computation.1 | async-start | bytes 7340032 | tf_op jit(solution)/shard_map/all_to_all | solution.py:87
  328.1 0.1 mul.73
  328.2 0.1 copy.47
  328.3 46.2 %all-to-all-done.1 = bf16[128,4,3584]{2,1,0:T(4,128)(2,1)} async-done(((bf16[128,4,3584]{2,1,0:T(4,128)(2,1)}), bf16[128,4,3584]{2,1,0:T(4,128)(2,1)}, u32[]{:S(2)}, u32[]{:S(2)}) %all-to-all-start.1) | async-done | bytes 3670048 | tf_op jit(solution)/shard_map/all_to_all | solution.py:87
  374.5 6.7 %reshape.117 = bf16[512,3584]{1,0:T(8,128)(2,1)} reshape(bf16[128,4,3584]{2,1,0:T(4,128)(2,1)} %all-to-all-done.1) | data formatting | bytes 7340032 | tf_op jit(solution)/shard_map/reshape | solution.py:90
  381.3 6.1 %gather_fusion = bf16[256,3584]{1,0:T(8,128)(2,1)S(1)} fusion(bf16[512,3584]{1,0:T(8,128)(2,1)} %reshape.117, s32[1024]{0:T(1024)S(1)} %pad_clamp_fusion), kind=kCustom, calls=%fused_computation | custom fusion | bytes 3671040 | tf_op jit(solution)/shard_map/gather | solution.py:91
  387.4 0.6 fusion.17
  388.0 1.7 fusion.23
  389.7 0.0 copy-done.1
  (16 shorter events, 0.1 us)
Async XLA Ops:
  6.5 107.1 %copy-start = (bf16[4,512,128]{2,1,0:T(8,128)(2,1)S(1)}, bf16[4,512,128]{2,1,0:T(8,128)(2,1)}, u32[]{:S(2)}) copy-start(bf16[4,512,128]{2,1,0:T(8,128)(2,1)} %param.14) | copy-start | bytes 1572868
  6.5 56.5 %all-gather.3.cloned.1.call-start = ((), (), s32[]{:S(2)}) async-start(), calls=%async_computation.2 | async-start | bytes 4177920 | tf_op jit(solution)/shard_map/all_gather | solution.py:29
  7.3 109.5 %all-gather.5.cloned.1.call-start = ((), (), s32[]{:S(2)}) async-start(), calls=%async_computation.3 | async-start | bytes 4128768 | tf_op jit(solution)/shard_map/all_gather | solution.py:53
  8.0 213.1 %all-reduce.2.cloned.1.call-start = ((), (), s32[]{:S(2)}) async-start(), calls=%async_computation.4 | async-start | bytes 7340032 | tf_op jit(solution)/shard_map/psum | solution.py:57
  116.8 6.1 %copy-start.4 = (s32[32,8]{0,1:T(8,128)S(1)}, s32[32,8]{0,1:T(8,128)}, u32[]{:S(2)}) copy-start(s32[32,8]{0,1:T(8,128)} %param.18) | copy-start | bytes 3076
  122.8 98.3 %copy-start.2 = (bf16[32,3584]{1,0:T(8,128)(2,1)S(1)}, bf16[32,3584]{1,0:T(8,128)(2,1)}, u32[]{:S(2)}) copy-start(bf16[32,3584]{1,0:T(8,128)(2,1)} %param.16) | copy-start | bytes 688132
  122.8 99.5 %copy-start.3 = (f32[3584]{0:T(1024)S(1)}, f32[3584]{0:T(1024)}, u32[]{:S(2)}) copy-start(f32[3584]{0:T(1024)} %param.17) | copy-start | bytes 43012
  323.0 5.1 %copy-start.5 = (f32[32,8]{0,1:T(8,128)S(1)}, f32[32,8]{0,1:T(8,128)}, u32[]{:S(2)}) copy-start(f32[32,8]{0,1:T(8,128)} %param.19) | copy-start | bytes 3076
  323.0 51.5 %all-to-all-start.1 = ((bf16[128,4,3584]{2,1,0:T(4,128)(2,1)}), bf16[128,4,3584]{2,1,0:T(4,128)(2,1)}, u32[]{:S(2)}, u32[]{:S(2)}) async-start(bf16[128,4,3584]{2,1,0:T(4,128)(2,1)} %reshape.116), calls=%async_computation.1 | async-start | bytes 7340032 | tf_op jit(solution)/shard_map/all_to_all | solution.py:87
  381.3 8.4 %copy-start.1 = (bf16[4,512,128]{2,1,0:T(8,128)(2,1)S(1)}, bf16[4,512,128]{2,1,0:T(8,128)(2,1)}, u32[]{:S(2)}) copy-start(bf16[4,512,128]{2,1,0:T(8,128)(2,1)} %param.14) | copy-start | bytes 1572868
Sparse Core Ops, SparseCore 0:
  9.5 53.4 all-gather.2
  64.7 30.2 all-gather.4
  123.0 98.1 all-reduce.1
where the time goes:
time: 398 us; the launch traced here: 396 us
  waiting for transfers between devices  193 us (48%)
  matrix products  67.3 us (17%)
  blocking collectives  55.2 us (14%)
  local copies, waits for them, and re-layouts  44.7 us (11%)
  other arithmetic  16.6 us (4%)
  between operations  13.9 us (3%)
  starting transfers between devices  5.11 us (1%)
    psum x1, waiting for transfers between devices, shards(): lax.psum(partial_value.astype(jnp.bfloat16), 'tensor').astype(jnp.float32)  97 us
    all_to_all x1, blocking collectives, shards(): lax.all_to_all(outgoing, ('dp', 'tensor'), split_axis=0, concat_axis=0, t...  55.2 us
    all_gather x1, waiting for transfers between devices, shards(): key_rows = lax.all_gather(cache, 'tensor', axis=1, tiled=True)[0]  48.7 us
    all_to_all x1, waiting for transfers between devices, shards(): lax.all_to_all(expert_out.reshape(row_shape), ('dp', 'tensor'), split_axi...  46.2 us
    dot_general x1, matrix products, shards(): jnp.einsum('thc,kc->htk', query_heads, key_rows, preferred_element_type=j...  18.4 us
    dot_general x1, matrix products, shards(): jnp.einsum('htk,kc->htc', weights.astype(jnp.bfloat16), key_rows[:, :late...  14.4 us
    dot_general x1, matrix products, shards(): jnp.dot(flat_rows, expert_in[0], preferred_element_type=jnp.float32)  12.1 us
    reduce_sum x1, other arithmetic, shards(): totals = jnp.sum(weights, axis=2)  11.7 us
  transfers between devices with their start and end apart: 4, of which 3 were waited for; matrix products, arithmetic and copies ran while one was open for 15% of the time, Pallas kernels for 0%

commit v1 on v0

--- a/solution.py
+++ b/solution.py
@@ -54,7 +54,9 @@
         preferred_element_type=jnp.float32,
     )
     tok_dev = resid.shape[0]
-    summed_all = lax.psum(partial_value.astype(jnp.bfloat16), "tensor").astype(jnp.float32)
+    summed_all = jnp.sum(
+        lax.all_gather(partial_value.astype(jnp.bfloat16), "tensor"), axis=0
+    ).astype(jnp.float32)
     attn_rows = lax.dynamic_slice_in_dim(summed_all, lax.axis_index("tensor") * tok_dev, tok_dev, 0)
     stream = resid.astype(jnp.float32) + attn_rows
     mean_square = jnp.mean(stream * stream, axis=1, keepdims=True)

time: 398 us -> 646 us (1.62)
  waiting for transfers between devices: 193 us -> 421 us
  other arithmetic: 16.6 us -> 38 us
    all_gather x0 -> x1, waiting for transfers between devices: none -> 324 us  [shards(): lax.all_gather(partial_value.astype(jnp.bfloat16), 'tensor')]
    psum x1 -> x0, waiting for transfers between devices: 97 us -> none  [shards(): lax.psum(partial_value.astype(jnp.bfloat16), 'tensor').astype(jnp.float32)]
    reduce_sum x0 -> x1, other arithmetic: none -> 21.4 us  [shards(): jnp.sum(lax.all_gather(partial_value.astype(jnp.bfloat16), 'tensor'), axi...]
  transfers between devices with their start and end apart: 4 -> 4, of which waited for: 3 -> 3; matrix products, arithmetic and copies ran while one was open for 15% -> 9% of each run, Pallas kernels for 0% -> 0%
where the time goes in v1:
time: 646 us; the launch traced here: 645 us
  waiting for transfers between devices  421 us (65%)
  matrix products  67.1 us (10%)
  blocking collectives  55.2 us (9%)
  local copies, waits for them, and re-layouts  44.7 us (7%)
  other arithmetic  38 us (6%)
  between operations  13.9 us (2%)
    all_gather x1, waiting for transfers between devices, shards(): lax.all_gather(partial_value.astype(jnp.bfloat16), 'tensor')  324 us
    all_to_all x1, blocking collectives, shards(): lax.all_to_all(outgoing, ('dp', 'tensor'), split_axis=0, concat_axis=0, t...  55.2 us
    all_gather x1, waiting for transfers between devices, shards(): key_rows = lax.all_gather(cache, 'tensor', axis=1, tiled=True)[0]  48.7 us
    all_to_all x1, waiting for transfers between devices, shards(): lax.all_to_all(expert_out.reshape(row_shape), ('dp', 'tensor'), split_axi...  46.5 us
    reduce_sum x1, other arithmetic, shards(): jnp.sum(lax.all_gather(partial_value.astype(jnp.bfloat16), 'tensor'), axi...  21.4 us
    dot_general x1, matrix products, shards(): jnp.einsum('thc,kc->htk', query_heads, key_rows, preferred_element_type=j...  18.4 us
    dot_general x1, matrix products, shards(): jnp.einsum('htk,kc->htc', weights.astype(jnp.bfloat16), key_rows[:, :late...  14.4 us
  transfers between devices with their start and end apart: 4, of which 3 were waited for; matrix products, arithmetic and copies ran while one was open for 9% of the time, Pallas kernels for 0%

profile of v1, /device:TPU:1, one launch (start us, length us, event | category | flops | bytes accessed | tf_op | source)
XLA Modules:
  0.0 644.5 jit_solution(16211505197439905512)
XLA Ops:
  6.5 0.0 copy-start
  6.5 0.0 all-gather.5.cloned.1.call-start
  6.5 0.7 all-gather.5.cloned.1.call-update
  7.3 0.0 all-gather.7.cloned.1.call-start
  7.3 0.7 all-gather.7.cloned.1.call-update
  8.0 0.0 all-gather.9.cloned.1.call-start
  8.7 1.3 iota_compare_fusion
  10.0 4.3 copy.35
  14.3 48.7 %all-gather.5.cloned.1.call-done = bf16[1,3072,576]{2,1,0:T(8,128)(2,1)} async-done(((bf16[1,192,576]{2,1,0:T(8,128)(2,1)}), bf16[1,3072,576]{2,1,0:T(8,128)(2,1)}) %all-gather.5.cloned.1.call-update) | async-done | bytes 3538960 | tf_op jit(solution)/shard_map/all_gather | solution.py:29
  63.0 18.4 %fusion = (f32[4,512]{1,0:T(4,128)S(1)}, f32[3072,512,4]{1,0,2:T(8,128)}) fusion(pred[512,3072]{0,1:T(8,128)(4,1)S(1)} %iota_compare_fusion, bf16[512,4,576]{0,2,1:T(8,128)(2,1)} %bitcast.63, bf16[1,3072,576]{2,1,0:T(8,128)(2,1)} %all-gather.5.cloned.1.call-done), kind=kOutput, calls=%fused_computation.3 | convolution fusion | flops 7266629632 | bytes 32645120 | tf_op jit(solution)/shard_map/thc,kc->htk/dot_general | solution.py:32
  81.4 6.1 copy.34
  87.5 11.7 %fusion.1 = f32[4,512]{1,0:T(4,128)S(1)} fusion(f32[3072,512,4]{1,0,2:T(8,128)} %get-tuple-element.8, f32[4,512]{1,0:T(4,128)S(1)} %broadcast_maximum_fusion, pred[512,3072]{0,1:T(8,128)(4,1)S(1)} %iota_compare_fusion), kind=kLoop, calls=%fused_computation.4 | loop fusion | flops 31455232 | bytes 26755072 | tf_op jit(solution)/shard_map/reduce_sum | solution.py:40
  99.2 14.4 %fusion.5 = f32[4,512,512]{2,1,0:T(8,128)} fusion(f32[3072,512,4]{1,0,2:T(8,128)} %get-tuple-element.8, f32[4,512]{1,0:T(4,128)S(1)} %broadcast_maximum_fusion, pred[512,3072]{0,1:T(8,128)(4,1)S(1)} %iota_compare_fusion, bf16[3072,576]{0,1:T(8,128)(2,1)} %bitcast.62), kind=kOutput, calls=%fused_computation.8 | convolution fusion | flops 6473908224 | bytes 34086912 | tf_op jit(solution)/shard_map/htk,kc->htc/dot_general | solution.py:41
  113.7 0.0 copy-done
  113.7 3.1 fusion.19
  116.8 0.0 all-gather.7.cloned.1.call-done
  116.8 0.0 copy-start.4
  116.8 6.0 convolution_convert_fusion.1
  122.8 0.0 all-gather.9.cloned.1.call-update
  122.8 0.0 copy-done.4
  122.8 0.1 copy.39
  122.9 0.1 eq.43
  123.0 0.1 eq.39
  123.1 0.1 copy.42
  123.2 0.2 fusion.27
  123.4 0.1 add_add_fusion
  123.5 0.2 fusion.28
  123.7 0.1 reduce_sum.46
  123.8 0.2 fusion.22
  124.0 324.1 %all-gather.9.cloned.1.call-done = bf16[8192,3584]{1,0:T(8,128)(2,1)} async-done(((bf16[512,3584]{1,0:T(8,128)(2,1)}), bf16[8192,3584]{1,0:T(8,128)(2,1)}) %all-gather.9.cloned.1.call-update) | async-done | bytes 58720272 | tf_op jit(solution)/shard_map/all_gather | solution.py:58
  448.2 21.4 %reduce_sum.44 = bf16[512,3584]{1,0:T(8,128)(2,1)} reduce(bf16[16,512,3584]{2,1,0:T(8,128)(2,1)} %bitcast.61, bf16[]{:T(256)} %constant.19.clone.1), dimensions={0}, to_apply=%region_2.3 | reduce | flops 27525120 | bytes 62390272 | tf_op jit(solution)/shard_map/reduce_sum | solution.py:57
  469.6 0.0 copy-done.2
  469.6 1.1 multiply_reduce_fusion
  470.7 4.0 convolution_convert_fusion
  474.7 7.0 %reshape.114 = bf16[128,4,3584]{2,1,0:T(4,128)(2,1)} reshape(bf16[512,3584]{1,0:T(8,128)(2,1)} %convolution_convert_fusion) | data formatting | bytes 7340032 | tf_op jit(solution)/shard_map/reshape | solution.py:78
  481.7 55.2 %all_to_all.10 = bf16[128,4,3584]{2,1,0:T(4,128)(2,1)} all-to-all(bf16[128,4,3584]{2,1,0:T(4,128)(2,1)} %reshape.114), channel_id=1, replica_groups=mesh['dp'=8,'tensor'=16] {'dp','tensor'}, dimensions={0} | all-to-all | bytes 7340032 | tf_op jit(solution)/shard_map/all_to_all | solution.py:79
  536.9 6.7 %reshape.115 = bf16[512,3584]{1,0:T(8,128)(2,1)} reshape(bf16[128,4,3584]{2,1,0:T(4,128)(2,1)} %all_to_all.10) | data formatting | bytes 7340032 | tf_op jit(solution)/shard_map/reshape | solution.py:81
  543.6 12.1 %fusion.3 = f32[512,2048]{1,0:T(8,128)S(1)} fusion(bf16[512,3584]{1,0:T(8,128)(2,1)} %reshape.115, bf16[1,3584,2048]{2,1,0:T(8,128)(2,1)} %param.20), kind=kOutput, calls=%fused_computation.6 | convolution fusion | flops 7516192768 | bytes 22544384 | tf_op jit(solution)/shard_map/dot_general | solution.py:82
  555.7 8.6 %fusion.10 = bf16[512,3584]{1,0:T(8,128)(2,1)} fusion(bf16[1,1024,3584]{2,1,0:T(8,128)(2,1)} %param.21, f32[512,2048]{1,0:T(8,128)S(1)} %fusion.3), kind=kOutput, calls=%fused_computation.13 | convolution fusion | flops 3763077120 | bytes 15204352 | tf_op jit(solution)/shard_map/dot_general | solution.py:86
  564.3 7.0 %reshape.116 = bf16[128,4,3584]{2,1,0:T(4,128)(2,1)} reshape(bf16[512,3584]{1,0:T(8,128)(2,1)} %fusion.10) | data formatting | bytes 7340032 | tf_op jit(solution)/shard_map/reshape | solution.py:90
  571.3 4.8 all-to-all-start.1
  576.2 0.1 mul.73
  576.3 0.1 copy.47
  576.4 46.5 %all-to-all-done.1 = bf16[128,4,3584]{2,1,0:T(4,128)(2,1)} async-done(((bf16[128,4,3584]{2,1,0:T(4,128)(2,1)}), bf16[128,4,3584]{2,1,0:T(4,128)(2,1)}, u32[]{:S(2)}, u32[]{:S(2)}) %all-to-all-start.1) | async-done | bytes 3670048 | tf_op jit(solution)/shard_map/all_to_all | solution.py:89
  622.8 6.7 %reshape.117 = bf16[512,3584]{1,0:T(8,128)(2,1)} reshape(bf16[128,4,3584]{2,1,0:T(4,128)(2,1)} %all-to-all-done.1) | data formatting | bytes 7340032 | tf_op jit(solution)/shard_map/reshape | solution.py:92
  629.6 6.1 gather_fusion
  635.7 0.6 fusion.17
  636.3 1.7 fusion.23
  (17 shorter events, 0.1 us)
Async XLA Ops:
  6.5 107.1 %copy-start = (bf16[4,512,128]{2,1,0:T(8,128)(2,1)S(1)}, bf16[4,512,128]{2,1,0:T(8,128)(2,1)}, u32[]{:S(2)}) copy-start(bf16[4,512,128]{2,1,0:T(8,128)(2,1)} %param.14) | copy-start | bytes 1572868
  6.5 56.5 %all-gather.5.cloned.1.call-start = ((), (), s32[]{:S(2)}) async-start(), calls=%async_computation.2 | async-start | bytes 4177920 | tf_op jit(solution)/shard_map/all_gather | solution.py:29
  7.3 109.5 %all-gather.7.cloned.1.call-start = ((), (), s32[]{:S(2)}) async-start(), calls=%async_computation.3 | async-start | bytes 4128768 | tf_op jit(solution)/shard_map/all_gather | solution.py:53
  8.0 440.1 %all-gather.9.cloned.1.call-start = ((), (), s32[]{:S(2)}) async-start(), calls=%async_computation.4 | async-start | bytes 62390272 | tf_op jit(solution)/shard_map/all_gather | solution.py:58
  116.8 6.0 copy-start.4
  448.2 21.4 %copy-start.2 = (bf16[32,3584]{1,0:T(8,128)(2,1)S(1)}, bf16[32,3584]{1,0:T(8,128)(2,1)}, u32[]{:S(2)}) copy-start(bf16[32,3584]{1,0:T(8,128)(2,1)} %param.16) | copy-start | bytes 688132
  448.2 22.6 %copy-start.3 = (f32[3584]{0:T(1024)S(1)}, f32[3584]{0:T(1024)}, u32[]{:S(2)}) copy-start(f32[3584]{0:T(1024)} %param.17) | copy-start | bytes 43012
  571.3 4.9 copy-start.5
  571.3 51.5 %all-to-all-start.1 = ((bf16[128,4,3584]{2,1,0:T(4,128)(2,1)}), bf16[128,4,3584]{2,1,0:T(4,128)(2,1)}, u32[]{:S(2)}, u32[]{:S(2)}) async-start(bf16[128,4,3584]{2,1,0:T(4,128)(2,1)} %reshape.116), calls=%async_computation.1 | async-start | bytes 7340032 | tf_op jit(solution)/shard_map/all_to_all | solution.py:89
  629.6 8.4 %copy-start.1 = (bf16[4,512,128]{2,1,0:T(8,128)(2,1)S(1)}, bf16[4,512,128]{2,1,0:T(8,128)(2,1)}, u32[]{:S(2)}) copy-start(bf16[4,512,128]{2,1,0:T(8,128)(2,1)} %param.14) | copy-start | bytes 1572868
Sparse Core Ops, SparseCore 0:
  9.5 53.4 all-gather.4
  64.7 30.2 all-gather.6
  122.9 325.1 all-gather.8
